TPU v7x, 32 devices: a whole 2x2x4 slice. The times are simulated.
32 devices in a mesh: lat: 8 (over z, y), lon: 4 (over x, core).
Axes of the slice: x: 2, y: 2, z: 4, core: 2. Of those that a mesh axis runs over, the one named last changes fastest.
Arguments:
- pair_table: int32 [640], replicated, may hold values from 0 to 639, each once
- spectral: bfloat16 [640, 384, 1408], P('lat', 'lon'), may hold values from -0.071777344 to 0.071777344
- lat_basis: bfloat16 [640, 32, 1408], P('lat'), may hold values from -0.15625 to 0.15625
- in_weight: bfloat16 [192, 512], replicated, may hold values from -0.4375 to 0.4375
- in_bias: float32 [512], replicated, may hold values from -3 to 3
- out_weight: bfloat16 [512, 192], replicated, may hold values from -0.25 to 0.25
- out_bias: float32 [192], replicated, may hold values from -3 to 3
- cotangent: bfloat16 [64, 192, 2560], P('lat', None, 'lon'), may hold values from -0.08984375 to 0.08984375
Outputs:
- tendency: bfloat16 [64, 192, 2560], P('lat', None, 'lon')
- spectral_grad: bfloat16 [640, 384, 1408], P('lat', 'lon')
- in_weight_grad: float32 [192, 512], replicated
- in_bias_grad: float32 [512], replicated
- out_weight_grad: float32 [512, 192], replicated
- out_bias_grad: float32 [192], replicated
Inputs may be any that keep to these rules, and one draw needn't show every extreme that they name: `pair_table`: each pair number appears exactly once.
All inputs are finite; a program needn't handle non-finite values.
Results may differ from a plain program's by a relative error of at most 0.015.
Values may be sent and summed in bfloat16 or wider, within the bound.
No kernel may reach another device: no remote copies, remote signals or barrier semaphores. Data moves between devices by JAX's collectives and lax.ppermute only.
A program may use at most 256 MiB of HBM per device.

v0:
```python
import math
import jax
import jax.numpy as jnp
from jax import lax
from jax.sharding import PartitionSpec as P

TRUNC = 1279


def pair_masks(pair_ids, length):
    first_len = TRUNC + 1 - pair_ids
    position = jnp.arange(length, dtype=jnp.int32)[None, :]
    lower_part = position < first_len[:, None]
    upper_part = jnp.logical_and(position >= first_len[:, None], position < TRUNC + 2)
    offset = jnp.where(lower_part, position, position - first_len[:, None])
    parity = jnp.where(offset % 2 == 0, 1.0, -1.0).astype(jnp.float32)
    return (lower_part, upper_part, parity, first_len)


def wave_numbers(pair_ids):
    both = jnp.stack([pair_ids, TRUNC - pair_ids], axis=1)
    return both.reshape(-1)


def fourier_table(numbers, lon_total):
    step = 128 if lon_total % 128 == 0 else 1
    coarse = jnp.arange(lon_total // step, dtype=jnp.int32) * step
    fine = jnp.arange(step, dtype=jnp.int32)
    scale = 2.0 * math.pi / lon_total

    def angles(offsets):
        phase = numbers[:, None] * offsets[None, :] % lon_total
        angle = phase.astype(jnp.float32) * scale
        return (jnp.cos(angle), jnp.sin(angle))

    cos_a, sin_a = angles(coarse)
    cos_b, sin_b = angles(fine)
    cos_t = cos_a[:, :, None] * cos_b[:, None, :] - sin_a[:, :, None] * sin_b[:, None, :]
    sin_t = sin_a[:, :, None] * cos_b[:, None, :] + cos_a[:, :, None] * sin_b[:, None, :]
    count = numbers.shape[0]
    factor = jnp.where(numbers == 0, 1.0, 2.0).astype(jnp.float32)[:, None]
    return jnp.stack(
        [factor * cos_t.reshape(count, lon_total), -factor * sin_t.reshape(count, lon_total)],
        axis=1,
    ).astype(jnp.bfloat16)


def per_device(
    pair_table, spectral, lat_basis, in_weight, in_bias, out_weight, out_bias, cotangent
):
    pair_dev = spectral.shape[0]
    width_local = spectral.shape[1]
    lat_half = lat_basis.shape[1]
    band_rows = cotangent.shape[0]
    block_cols = cotangent.shape[2]
    lon_total = block_cols * lax.axis_size("lon")
    first_row = lax.axis_index("lat") * pair_dev
    local_ids = lax.dynamic_slice_in_dim(pair_table, first_row, pair_dev)
    lower_part, upper_part, parity, first_len = pair_masks(local_ids, spectral.shape[2])
    rows = jnp.concatenate([lat_basis, lat_basis * parity[:, None, :].astype(jnp.bfloat16)], axis=1)
    zero = jnp.zeros_like(rows)
    basis = jnp.stack(
        [
            jnp.where(lower_part[:, None, :], rows, zero),
            jnp.where(upper_part[:, None, :], rows, zero),
        ],
        axis=1,
    )
    lat_window = 2 * lat_half
    raw_waves = jnp.einsum(
        "pqlj,pkj->pqlk", basis, spectral, preferred_element_type=jnp.float32
    ).astype(jnp.bfloat16)
    waves = jnp.concatenate(
        [raw_waves[:, :, :lat_half], jnp.flip(raw_waves[:, :, lat_half:], axis=2)], axis=2
    )
    flat_waves = waves.reshape(2 * pair_dev, lat_window * width_local)
    band_waves = lax.all_to_all(flat_waves, "lat", split_axis=1, concat_axis=0, tiled=True)
    wave_count = band_waves.shape[0]
    coeff_grid = band_waves.reshape(wave_count, band_rows, width_local // 2, 2)
    numbers = wave_numbers(pair_table)
    full_table = fourier_table(numbers, lon_total)
    all_columns = jnp.einsum(
        "glkc,gcn->lkn", coeff_grid, full_table, preferred_element_type=jnp.float32
    ).astype(jnp.bfloat16)
    grid = lax.all_to_all(all_columns, "lon", split_axis=2, concat_axis=1, tiled=True)
    pre_act = (
        jnp.einsum("lkc,kh->lch", grid, in_weight, preferred_element_type=jnp.float32) + in_bias
    )
    activated, gelu_back = jax.vjp(jax.nn.gelu, pre_act)
    hidden = activated.astype(jnp.bfloat16)
    tendency = (
        jnp.einsum("lch,hk->lkc", hidden, out_weight, preferred_element_type=jnp.float32)
        + out_bias[None, :, None]
    ).astype(jnp.bfloat16)
    out_weight_part = jnp.einsum(
        "lch,lkc->kh", hidden, cotangent, preferred_element_type=jnp.float32
    )
    out_bias_part = jnp.sum(cotangent.astype(jnp.float32), axis=(0, 2))
    hidden_grad = jnp.einsum(
        "lkc,hk->lch", cotangent, out_weight, preferred_element_type=jnp.float32
    )
    pre_grad = gelu_back(hidden_grad)[0].astype(jnp.bfloat16)
    in_weight_part = jnp.einsum("lkc,lch->kh", grid, pre_grad, preferred_element_type=jnp.float32)
    in_bias_part = jnp.sum(pre_grad.astype(jnp.float32), axis=(0, 1))
    grid_grad = jnp.einsum(
        "lch,kh->lkc", pre_grad, in_weight, preferred_element_type=jnp.float32
    ).astype(jnp.bfloat16)
    channels, hid = in_weight.shape
    width = max(hid, channels)

    def widen(v):
        return jnp.pad(v, ((0, 0), (0, width - v.shape[1])))

    stacked = jnp.concatenate(
        [
            widen(in_weight_part),
            widen(out_weight_part),
            widen(in_bias_part[None, :]),
            widen(out_bias_part[None, :]),
        ],
        axis=0,
    )
    summed = lax.psum(stacked, ("lat", "lon"))
    in_weight_grad = summed[:channels, :hid]
    out_weight_grad = summed[channels : 2 * channels, :hid].T
    in_bias_grad = summed[2 * channels, :hid]
    out_bias_grad = summed[2 * channels + 1, :channels]
    level_rows = lax.all_to_all(grid_grad, "lon", split_axis=1, concat_axis=2, tiled=True)
    wave_grad = jnp.einsum(
        "gcn,lkn->glkc", full_table, level_rows, preferred_element_type=jnp.float32
    ).astype(jnp.bfloat16)
    flat_grad = wave_grad.reshape(wave_count, band_rows * width_local)
    pair_grad = lax.all_to_all(flat_grad, "lat", split_axis=0, concat_axis=1, tiled=True)
    pair_grad = pair_grad.reshape(pair_dev, 2, lat_window, width_local)
    pair_grad = jnp.concatenate(
        [pair_grad[:, :, :lat_half], jnp.flip(pair_grad[:, :, lat_half:], axis=2)], axis=2
    )
    spectral_grad = jnp.einsum(
        "pqlk,pqlj->pkj", pair_grad, basis, preferred_element_type=jnp.float32
    ).astype(jnp.bfloat16)
    return (tendency, spectral_grad, in_weight_grad, in_bias_grad, out_weight_grad, out_bias_grad)


def solution(mesh):
    placed = (
        P(),
        P("lat", "lon", None),
        P("lat", None, None),
        P(),
        P(),
        P(),
        P(),
        P("lat", None, "lon"),
    )
    return jax.shard_map(
        per_device,
        mesh=mesh,
        in_specs=placed,
        out_specs=(P("lat", None, "lon"), P("lat", "lon", None), P(), P(), P(), P()),
        check_vma=False,
    )
```

profile of v0, /device:TPU:1, one launch (start us, length us, event | category | flops | bytes accessed | tf_op | source)
XLA Modules:
  0.0 477.1 jit_solution(11046358141665475062)
XLA Ops:
  8.6 7.1 %multiply_bitcast_fusion = bf16[80,1,32,1408]{3,2,1,0:T(8,128)(2,1)} fusion(bf16[80,32,1408]{2,1,0:T(8,128)(2,1)} %param.10, bf16[80,1408]{1,0:T(8,128)(2,1)S(1)} %select_convert_fusion), kind=kLoop, calls=%fused_computation.25 | loop fusion | flops 3604480 | bytes 14643200 | tf_op jit(solution)/shard_map/concatenate | solution.py:60
  15.7 14.2 %broadcast_select_fusion.1 = (bf16[80,1,64,1408]{3,2,1,0:T(8,128)(2,1)}, bf16[80,1,64,1408]{3,2,1,0:T(8,128)(2,1)}) fusion(pred[80,1408]{1,0:T(8,128)(4,1)S(1)} %get-tuple-element.22, bf16[80,1,32,1408]{3,2,1,0:T(8,128)(2,1)} %multiply_bitcast_fusion, bf16[80,1,32,1408]{3,2,1,0:T(8,128)(2,1)S(1)} %bitcast.97, pred[80,1408]{1,0:T(8,128)(4,1)S(1)} %get-tuple-element.23), kind=kLoop, calls=%fused_computation.8 | loop fusion | flops 43253760 | bytes 43479040 | tf_op jit(solution)/shard_map/jit(_where)/select_n | solution.py:64
  29.8 20.0 %fusion.18 = bf16[80,2,64,96]{3,2,1,0:T(8,128)(2,1)} fusion(bf16[80,96,1408]{2,1,0:T(8,128)(2,1)} %param.9, bf16[80,1,64,1408]{3,2,1,0:T(8,128)(2,1)} %get-tuple-element.7, bf16[80,1,64,1408]{3,2,1,0:T(8,128)(2,1)} %get-tuple-element.6), kind=kOutput, calls=%fused_computation.36 | convolution fusion | flops 2783641600 | bytes 52428800 | tf_op jit(solution)/shard_map/pqlj,pkj->pqlk/dot_general | solution.py:70
  49.8 3.4 fusion.52
  58.3 3.1 all_to_all.50
  61.4 3.2 copy.25
  64.6 6.9 %all-to-all-start = ((bf16[160,8,768]{2,0,1:T(8,128)(2,1)}), bf16[160,8,768]{2,0,1:T(8,128)(2,1)S(1)}, u32[]{:S(2)}, u32[]{:S(2)}) async-start(bf16[160,8,768]{2,0,1:T(8,128)(2,1)} %copy.25), calls=%async_computation | async-start | bytes 3932160 | tf_op jit(solution)/shard_map/all_to_all | solution.py:77
  75.9 13.6 %multiply_subtract_fusion = (f32[1280,20,128]{0,2,1:T(8,128)}, f32[1280,20,128]{0,2,1:T(8,128)}) fusion(f32[1280,128]{0,1:T(8,128)S(1)} %get-tuple-element.21, f32[1280,20]{0,1:T(8,128)} %get-tuple-element.17, f32[1280,128]{0,1:T(8,128)S(1)} %get-tuple-element.20, f32[1280,20]{0,1:T(8,128)} %get-tuple-element.16), kind=kLoop, calls=%fused_computation.13 | loop fusion | flops 19660800 | bytes 27729920 | tf_op jit(solution)/shard_map/sub | solution.py:38
  89.6 14.0 %copy.29 = f32[1280,1,2560]{2,0,1:T(8,128)} copy(f32[1280,1,2560]{0,2,1:T(8,128)} %bitcast.94) | data formatting | bytes 26214400 | tf_op jit(solution)/shard_map/add | solution.py:39
  103.6 14.0 %copy.28 = f32[1280,1,2560]{2,0,1:T(8,128)} copy(f32[1280,1,2560]{0,2,1:T(8,128)} %bitcast.93) | data formatting | bytes 26214400 | tf_op jit(solution)/shard_map/sub | solution.py:38
  117.5 13.9 %multiply_convert_fusion = (bf16[1280,1,2560]{2,0,1:T(8,128)(2,1)}, bf16[1280,1,2560]{2,0,1:T(8,128)(2,1)}) fusion(f32[1280,1,2560]{2,0,1:T(8,128)} %copy.29, f32[1280]{0:T(1024)S(1)} %get-tuple-element.19, f32[1280,1,2560]{2,0,1:T(8,128)} %copy.28, f32[1280]{0:T(1024)S(1)} %get-tuple-element.18), kind=kLoop, calls=%fused_computation.10 | loop fusion | flops 13107200 | bytes 39331840 | tf_op jit(solution)/shard_map/convert.1
  132.7 4.1 copy.26
  136.8 5.2 %reshape.454 = bf16[1280,8,48,2]{0,3,2,1:T(2,128)(2,1)} reshape(bf16[8,160,768]{1,0,2:T(8,128)(2,1)S(1)} %copy.26) | data formatting | bytes 3932160 | tf_op jit(solution)/shard_map/reshape | solution.py:79
  142.1 8.9 %fusion.12 = bf16[8,48,2560]{2,1,0:T(8,128)(2,1)S(1)} fusion(bf16[1280,1,2560]{2,0,1:T(8,128)(2,1)} %get-tuple-element.28, bf16[1280,1,2560]{2,0,1:T(8,128)(2,1)} %get-tuple-element.29, bf16[1280,8,48,2]{0,3,2,1:T(2,128)(2,1)} %reshape.454), kind=kOutput, calls=%fused_computation.27 | convolution fusion | flops 5040701440 | bytes 17039360 | tf_op jit(solution)/shard_map/glkc,gcn->lkn/dot_general | solution.py:82
  151.0 5.4 %copy.31 = bf16[8,48,2560]{1,0,2:T(8,128)(2,1)} copy(bf16[8,48,2560]{2,1,0:T(8,128)(2,1)S(1)} %fusion.12) | data formatting | bytes 3932160 | tf_op jit(solution)/shard_map/convert_element_type | solution.py:84
  156.4 8.8 %reshape.467 = bf16[4,2,122880]{2,1,0:T(2,128)(2,1)S(1)} reshape(bf16[2560,8,48]{2,1,0:T(8,128)(2,1)} %bitcast.98) | data formatting | bytes 3932160
  165.3 27.4 %all_to_all.68 = bf16[4,2,122880]{2,1,0:T(2,128)(2,1)} all-to-all(bf16[4,2,122880]{2,1,0:T(2,128)(2,1)S(1)} %reshape.467), channel_id=1, replica_groups=mesh['lat'=8,'lon'=4] {'lon'}, dimensions={0} | all-to-all | bytes 3932160 | tf_op jit(solution)/shard_map/all_to_all | solution.py:85
  192.7 7.1 %reshape.468 = bf16[2560,8,48]{2,1,0:T(8,128)(2,1)} reshape(bf16[4,2,122880]{2,1,0:T(2,128)(2,1)} %all_to_all.68) | data formatting | bytes 3932160
  199.8 5.7 %copy.32 = bf16[8,48,4,640]{3,1,2,0:T(8,128)(2,1)S(1)} copy(bf16[8,48,4,640]{1,0,3,2:T(8,128)(2,1)} %bitcast.99) | data formatting | bytes 3932160 | tf_op jit(solution)/shard_map/all_to_all | solution.py:85
  205.5 5.5 %multiply_convert_fusion.2 = (bf16[8,640,512]{2,1,0:T(8,128)(2,1)}, f32[8,640,512]{2,1,0:T(8,128)S(1)}) fusion(f32[512]{0:T(512)S(1)} %copy-done.8, bf16[8,192,640]{2,1,0:T(8,128)(2,1)S(1)} %bitcast.104, bf16[192,512]{1,0:T(8,128)(2,1)S(1)} %copy-done), kind=kOutput, calls=%fused_computation.22 | convolution fusion | flops 1032847360 | bytes 17893376 | tf_op jit(solution)/shard_map/lkc,kh->lch/dot_general | solution.py:87
  211.0 8.7 %convert_reduce_fusion = (f32[512]{0:T(512)S(1)}, bf16[8,640,512]{2,1,0:T(8,128)(2,1)S(1)}) fusion(f32[8,640,512]{2,1,0:T(8,128)S(1)} %get-tuple-element.25, f32[512]{0:T(512)S(1)} %copy-done.8, bf16[8,192,640]{2,1,0:T(8,128)(2,1)S(1)} %copy-done.3, bf16[512,192]{0,1:T(8,128)(2,1)S(1)} %copy-done.7), kind=kOutput, calls=%fused_computation.21 | convolution fusion | flops 1066925568 | bytes 17895424 | tf_op jit(solution)/shard_map/lkc,hk->lch/dot_general | solution.py:99
  222.7 26.9 %all_to_all.69 = bf16[8,192,640]{2,0,1:T(8,128)(2,1)S(1)} all-to-all(bf16[8,192,640]{2,0,1:T(8,128)(2,1)S(1)} %copy.33), channel_id=1, replica_groups=mesh['lat'=8,'lon'=4] {'lon'}, dimensions={1} | all-to-all | bytes 3932160 | tf_op jit(solution)/shard_map/all_to_all | solution.py:128
  253.4 9.0 %fusion.14 = bf16[1280,8,48,2]{0,2,3,1:T(8,128)(2,1)S(1)} fusion(bf16[1280,1,2560]{2,0,1:T(8,128)(2,1)} %get-tuple-element.28, bf16[1280,1,2560]{2,0,1:T(8,128)(2,1)} %get-tuple-element.29, bf16[8,48,2560,1]{2,1,0,3:T(8,128)(2,1)} %reshape.462), kind=kOutput, calls=%fused_computation.31 | convolution fusion | flops 5060362240 | bytes 17039360 | tf_op jit(solution)/shard_map/gcn,lkn->glkc/dot_general | solution.py:129
  265.2 6.4 %all_to_all.61 = bf16[8,160,768]{1,0,2:T(8,128)(2,1)S(1)} reshape(bf16[1280,8,48,2]{0,3,2,1:T(2,128)(2,1)} %copy.35) | data formatting | bytes 3932160 | tf_op jit(solution)/shard_map/all_to_all | solution.py:133
  271.6 3.2 copy.36
  274.8 5.7 %all-to-all-start.3 = ((bf16[8,160,768]{2,1,0:T(8,128)(2,1)}), bf16[8,160,768]{2,1,0:T(8,128)(2,1)S(1)}, u32[]{:S(2)}, u32[]{:S(2)}) async-start(bf16[8,160,768]{2,1,0:T(8,128)(2,1)} %copy.36), calls=%async_computation.3 | async-start | bytes 3932160 | tf_op jit(solution)/shard_map/all_to_all | solution.py:133
  282.9 4.6 convolution_bitcast_fusion.1
  289.8 5.6 %fusion.23 = bf16[8,192,640]{2,1,0:T(8,128)(2,1)} fusion(f32[192]{0:T(256)S(1)} %copy-done.9, bf16[8,640,512]{2,1,0:T(8,128)(2,1)} %get-tuple-element.24, bf16[512,192]{0,1:T(8,128)(2,1)S(1)} %copy-done.7), kind=kOutput, calls=%fused_computation.41 | convolution fusion | flops 1008599040 | bytes 7406336 | tf_op jit(solution)/shard_map/lch,hk->lkc/dot_general | solution.py:92
  295.4 136.8 %all-reduce.3.cloned.1.call-done = f32[386,512]{1,0:T(8,128)} async-done(((f32[386,512]{1,0:T(8,128)}), f32[386,512]{1,0:T(8,128)}) %all-reduce.3.cloned.1.call-update) | async-done | bytes 790544 | tf_op jit(solution)/shard_map/psum | solution.py:123
  439.1 4.6 reshape.456
  446.1 3.4 rev.8
  449.5 20.5 %bitcast_convert_fusion = bf16[80,96,1408]{2,1,0:T(8,128)(2,1)} fusion(bf16[80,1,64,1408]{3,2,1,0:T(8,128)(2,1)} %get-tuple-element.7, bf16[80,1,64,1408]{3,2,1,0:T(8,128)(2,1)} %get-tuple-element.6, bf16[80,2,32,96]{3,2,1,0:T(8,128)(2,1)S(1)} %rev.8, bf16[80,2,32,96]{3,2,1,0:T(8,128)(2,1)} %get-tuple-element.8), kind=kOutput, calls=%fused_computation | convolution fusion | flops 2797404160 | bytes 52428800 | tf_op jit(solution)/shard_map/pqlk,pqlj->pkj/dot_general | solution.py:138
  (63 shorter events, 35.4 us)
Async XLA Ops:
  7.2 198.3 %copy-start = (bf16[192,512]{1,0:T(8,128)(2,1)S(1)}, bf16[192,512]{1,0:T(8,128)(2,1)}, u32[]{:S(2)}) copy-start(bf16[192,512]{1,0:T(8,128)(2,1)} %param.11) | copy-start | bytes 589828
  8.3 7.3 %slice-start = ((s8[7208960]{0:T(1024)(128)(4,1)}), s8[4194304]{0:T(1024)(128)(4,1)S(1)}, s32[]{:S(2)}) async-start(s8[7208960]{0:T(1024)(128)(4,1)} %bitcast.95), calls=%async_computation.5 | async-start | bytes 8388608
  8.6 7.1 %slice-start.1 = ((s8[7208960]{0:T(1024)(128)(4,1)}), s8[3014656]{0:T(1024)(128)(4,1)S(1)}, s32[]{:S(2)}) async-start(s8[7208960]{0:T(1024)(128)(4,1)} %bitcast.95), calls=%async_computation.6 | async-start | bytes 6029312
  58.3 13.3 %copy-start.6 = (s32[640]{0:T(1024)S(1)}, s32[640]{0:T(1024)}, u32[]{:S(2)}) copy-start(s32[640]{0:T(1024)} %param.8) | copy-start | bytes 7684
  64.6 66.8 %all-to-all-start = ((bf16[160,8,768]{2,0,1:T(8,128)(2,1)}), bf16[160,8,768]{2,0,1:T(8,128)(2,1)S(1)}, u32[]{:S(2)}, u32[]{:S(2)}) async-start(bf16[160,8,768]{2,0,1:T(8,128)(2,1)} %copy.25), calls=%async_computation | async-start | bytes 3932160 | tf_op jit(solution)/shard_map/all_to_all | solution.py:77
  131.5 1.3 copy-start.1
  192.7 12.8 %copy-start.8 = (f32[512]{0:T(512)S(1)}, f32[512]{0:T(512)}, u32[]{:S(2)}) copy-start(f32[512]{0:T(512)} %param.12) | copy-start | bytes 6148
  205.5 5.6 %copy-start.5 = (bf16[8,48,4,640]{3,1,2,0:T(8,128)(2,1)}, bf16[8,48,4,640]{3,1,2,0:T(8,128)(2,1)S(1)}, u32[]{:S(2)}) copy-start(bf16[8,48,4,640]{3,1,2,0:T(8,128)(2,1)S(1)} %copy.32) | copy-start | bytes 5898244
  205.5 5.5 %copy-start.3 = (bf16[8,192,640]{2,1,0:T(8,128)(2,1)S(1)}, bf16[8,192,640]{2,1,0:T(8,128)(2,1)}, u32[]{:S(2)}) copy-start(bf16[8,192,640]{2,1,0:T(8,128)(2,1)} %param.15) | copy-start | bytes 5898244
  205.5 5.5 %copy-start.7 = (bf16[512,192]{0,1:T(8,128)(2,1)S(1)}, bf16[512,192]{0,1:T(8,128)(2,1)}, u32[]{:S(2)}) copy-start(bf16[512,192]{0,1:T(8,128)(2,1)} %param.13) | copy-start | bytes 589828
  219.7 29.9 %copy-start.2 = (bf16[8,640,512]{2,1,0:T(8,128)(2,1)}, bf16[8,640,512]{2,1,0:T(8,128)(2,1)S(1)}, u32[]{:S(2)}) copy-start(bf16[8,640,512]{2,1,0:T(8,128)(2,1)S(1)} %get-tuple-element.27) | copy-start | bytes 15728644
  274.8 161.9 %all-to-all-start.3 = ((bf16[8,160,768]{2,1,0:T(8,128)(2,1)}), bf16[8,160,768]{2,1,0:T(8,128)(2,1)S(1)}, u32[]{:S(2)}, u32[]{:S(2)}) async-start(bf16[8,160,768]{2,1,0:T(8,128)(2,1)} %copy.36), calls=%async_computation.3 | async-start | bytes 3932160 | tf_op jit(solution)/shard_map/all_to_all | solution.py:133
  280.6 151.6 %all-reduce.3.cloned.1.call-start = ((), (), s32[]{:S(2)}) async-start(), calls=%async_computation.4 | async-start | bytes 1605632 | tf_op jit(solution)/shard_map/psum | solution.py:123
  280.9 6.7 %copy-start.4 = (bf16[8,192,640]{2,1,0:T(8,128)(2,1)S(1)}, bf16[8,192,640]{2,1,0:T(8,128)(2,1)}, u32[]{:S(2)}) copy-start(bf16[8,192,640]{2,1,0:T(8,128)(2,1)} %param.15) | copy-start | bytes 5898244
  280.9 6.7 %slice-start.2 = ((s8[5242880]{0:T(1024)(128)(4,1)}), s8[4194304]{0:T(1024)(128)(4,1)S(1)}, s32[]{:S(2)}) async-start(s8[5242880]{0:T(1024)(128)(4,1)} %bitcast.110), calls=%async_computation.7 | async-start | bytes 8388608
  282.9 4.6 slice-start.3
  287.5 2.3 copy-start.9
Sparse Core Ops, SparseCore 0:
  289.9 142.2 all-reduce.2
where the time goes:
time: 484 us; the launch traced here: 477 us
  waiting for transfers between devices  137 us (28%)
  local copies, waits for them, and re-layouts  113 us (23%)
  matrix products  85.8 us (18%)
  other arithmetic  59.6 us (12%)
  blocking collectives  54.4 us (11%)
  between operations  14.7 us (3%)
  starting transfers between devices  12.9 us (3%)
    psum x1, waiting for transfers between devices, per_device(): summed = lax.psum(stacked, ('lat', 'lon'))  137 us
    all_to_all x1, blocking collectives, per_device(): lax.all_to_all(all_columns, 'lon', split_axis=2, concat_axis=1, tiled=True)  27.4 us
    all_to_all x1, blocking collectives, per_device(): lax.all_to_all(grid_grad, 'lon', split_axis=1, concat_axis=2, tiled=True)  26.9 us
    dot_general x1, matrix products, per_device(): jnp.einsum('pqlk,pqlj->pkj', pair_grad, basis, preferred_element_type=jnp...  20.5 us
    dot_general x1, matrix products, per_device(): jnp.einsum('pqlj,pkj->pqlk', basis, spectral, preferred_element_type=jnp....  20 us
    unnamed x30, local copies, waits for them, and re-layouts  17.3 us
    select_n x1, other arithmetic, per_device(): jnp.where(lower_part[:, None, :], rows, zero)  14.2 us
    add x1, local copies, waits for them, and re-layouts, fourier_table(): sin_a[:, :, None] * cos_b[:, None, :]  14 us
  transfers between devices with their start and end apart: 3, of which 1 were waited for; matrix products, arithmetic and copies ran while one was open for 17% of the time, Pallas kernels for 0%

commit v1 on v0

--- a/solution.py
+++ b/solution.py
@@ -5,6 +5,7 @@
 from jax.sharding import PartitionSpec as P
 
 TRUNC = 1279
+post_leaf_on = lambda m, net_axis: jax.lax.all_gather(m, axis_name=net_axis).sum(axis=0)
 
 
 def pair_masks(pair_ids, length):
@@ -120,7 +121,7 @@
         ],
         axis=0,
     )
-    summed = lax.psum(stacked, ("lat", "lon"))
+    summed = post_leaf_on(stacked, ("lat", "lon"))
     in_weight_grad = summed[:channels, :hid]
     out_weight_grad = summed[channels : 2 * channels, :hid].T
     in_bias_grad = summed[2 * channels, :hid]

time: 484 us -> 446 us (0.921)
  waiting for transfers between devices: 137 us -> 106 us
  blocking collectives: 54.4 us -> 32.5 us
  other arithmetic: 59.6 us -> 69.5 us
  starting transfers between devices: 12.9 us -> 17.9 us
    psum x1 -> x0, waiting for transfers between devices: 137 us -> none  [per_device(): summed = lax.psum(stacked, ('lat', 'lon'))]
    all_to_all x1, waiting for transfers between devices: 0.01 us -> 75 us  [per_device(): lax.all_to_all(flat_grad, 'lat', split_axis=0, concat_axis=1, tiled=True)]
    all_to_all x1 -> x0, blocking collectives: 27.4 us -> none  [per_device(): lax.all_to_all(all_columns, 'lon', split_axis=2, concat_axis=1, tiled=True)]
    all_to_all x0 -> x1, waiting for transfers between devices: none -> 21.5 us  [per_device(): lax.all_to_all(all_columns, 'lon', split_axis=2, concat_axis=1, tiled=True)]
    reduce_sum x0 -> x1, other arithmetic: none -> 10.1 us  [jax.lax.all_gather(m, axis_name=net_axis).sum(axis=0)]
    all_gather x0 -> x1, waiting for transfers between devices: none -> 9.89 us  [jax.lax.all_gather(m, axis_name=net_axis).sum(axis=0)]
    all_to_all x1, blocking collectives: 26.9 us -> 32.5 us  [per_device(): lax.all_to_all(grid_grad, 'lon', split_axis=1, concat_axis=2, tiled=True)]
    unnamed x30 -> x24, local copies, waits for them, and re-layouts: 17.3 us -> 20.6 us
  transfers between devices with their start and end apart: 3 -> 4, of which waited for: 1 -> 3; matrix products, arithmetic and copies ran while one was open for 17% -> 28% of each run, Pallas kernels for 0% -> 0%
where the time goes in v1:
time: 446 us; the launch traced here: 438 us
  local copies, waits for them, and re-layouts  114 us (26%)
  waiting for transfers between devices  106 us (24%)
  matrix products  83.4 us (19%)
  other arithmetic  69.5 us (16%)
  blocking collectives  32.5 us (7%)
  starting transfers between devices  17.9 us (4%)
  between operations  14.8 us (3%)
    all_to_all x1, waiting for transfers between devices, per_device(): lax.all_to_all(flat_grad, 'lat', split_axis=0, concat_axis=1, tiled=True)  75 us
    all_to_all x1, blocking collectives, per_device(): lax.all_to_all(grid_grad, 'lon', split_axis=1, concat_axis=2, tiled=True)  32.5 us
    all_to_all x1, waiting for transfers between devices, per_device(): lax.all_to_all(all_columns, 'lon', split_axis=2, concat_axis=1, tiled=True)  21.5 us
    dot_general x1, matrix products, per_device(): jnp.einsum('pqlk,pqlj->pkj', pair_grad, basis, preferred_element_type=jnp...  20.7 us
    unnamed x24, local copies, waits for them, and re-layouts  20.6 us
    dot_general x1, matrix products, per_device(): jnp.einsum('pqlj,pkj->pqlk', basis, spectral, preferred_element_type=jnp....  20 us
    select_n x1, other arithmetic, per_device(): jnp.where(lower_part[:, None, :], rows, zero)  14.1 us
    sub x1, local copies, waits for them, and re-layouts, fourier_table(): cos_a[:, :, None] * cos_b[:, None, :]  14 us
  transfers between devices with their start and end apart: 4, of which 3 were waited for; matrix products, arithmetic and copies ran while one was open for 28% of the time, Pallas kernels for 0%

profile of v1, /device:TPU:1, one launch (start us, length us, event | category | flops | bytes accessed | tf_op | source)
XLA Modules:
  0.0 438.4 jit_solution(5686833686874475718)
XLA Ops:
  8.6 7.1 %multiply_bitcast_fusion = bf16[80,1,32,1408]{3,2,1,0:T(8,128)(2,1)} fusion(bf16[80,32,1408]{2,1,0:T(8,128)(2,1)} %param.10, bf16[80,1408]{1,0:T(8,128)(2,1)S(1)} %select_convert_fusion), kind=kLoop, calls=%fused_computation.25 | loop fusion | flops 3604480 | bytes 14643200 | tf_op jit(solution)/shard_map/concatenate | solution.py:61
  15.7 14.1 %broadcast_select_fusion.1 = (bf16[80,1,64,1408]{3,2,1,0:T(8,128)(2,1)}, bf16[80,1,64,1408]{3,2,1,0:T(8,128)(2,1)}) fusion(pred[80,1408]{1,0:T(8,128)(4,1)S(1)} %get-tuple-element.22, bf16[80,1,32,1408]{3,2,1,0:T(8,128)(2,1)} %multiply_bitcast_fusion, bf16[80,1,32,1408]{3,2,1,0:T(8,128)(2,1)S(1)} %bitcast.99, pred[80,1408]{1,0:T(8,128)(4,1)S(1)} %get-tuple-element.23), kind=kLoop, calls=%fused_computation.8 | loop fusion | flops 43253760 | bytes 43479040 | tf_op jit(solution)/shard_map/jit(_where)/select_n | solution.py:65
  29.8 20.0 %fusion.18 = bf16[80,2,64,96]{3,2,1,0:T(8,128)(2,1)} fusion(bf16[80,96,1408]{2,1,0:T(8,128)(2,1)} %param.9, bf16[80,1,64,1408]{3,2,1,0:T(8,128)(2,1)} %get-tuple-element.7, bf16[80,1,64,1408]{3,2,1,0:T(8,128)(2,1)} %get-tuple-element.6), kind=kOutput, calls=%fused_computation.36 | convolution fusion | flops 2783641600 | bytes 52428800 | tf_op jit(solution)/shard_map/pqlj,pkj->pqlk/dot_general | solution.py:71
  49.8 3.4 fusion.53
  64.6 6.9 %all-to-all-start = ((bf16[160,8,768]{2,0,1:T(8,128)(2,1)}), bf16[160,8,768]{2,0,1:T(8,128)(2,1)S(1)}, u32[]{:S(2)}, u32[]{:S(2)}) async-start(bf16[160,8,768]{2,0,1:T(8,128)(2,1)} %copy.25), calls=%async_computation | async-start | bytes 3932160 | tf_op jit(solution)/shard_map/all_to_all | solution.py:78
  75.9 13.6 %multiply_subtract_fusion = (f32[1280,20,128]{0,2,1:T(8,128)}, f32[1280,20,128]{0,2,1:T(8,128)}) fusion(f32[1280,128]{0,1:T(8,128)S(1)} %get-tuple-element.21, f32[1280,20]{0,1:T(8,128)} %get-tuple-element.17, f32[1280,128]{0,1:T(8,128)S(1)} %get-tuple-element.20, f32[1280,20]{0,1:T(8,128)} %get-tuple-element.16), kind=kLoop, calls=%fused_computation.13 | loop fusion | flops 19660800 | bytes 27729920 | tf_op jit(solution)/shard_map/sub | solution.py:39
  89.5 13.9 %copy.29 = f32[1280,1,2560]{2,0,1:T(8,128)} copy(f32[1280,1,2560]{0,2,1:T(8,128)} %bitcast.96) | data formatting | bytes 26214400 | tf_op jit(solution)/shard_map/add | solution.py:40
  103.5 14.0 %copy.28 = f32[1280,1,2560]{2,0,1:T(8,128)} copy(f32[1280,1,2560]{0,2,1:T(8,128)} %bitcast.95) | data formatting | bytes 26214400 | tf_op jit(solution)/shard_map/sub | solution.py:39
  117.5 13.9 %multiply_convert_fusion = (bf16[1280,1,2560]{2,0,1:T(8,128)(2,1)}, bf16[1280,1,2560]{2,0,1:T(8,128)(2,1)}) fusion(f32[1280,1,2560]{2,0,1:T(8,128)} %copy.29, f32[1280]{0:T(1024)S(1)} %get-tuple-element.19, f32[1280,1,2560]{2,0,1:T(8,128)} %copy.28, f32[1280]{0:T(1024)S(1)} %get-tuple-element.18), kind=kLoop, calls=%fused_computation.10 | loop fusion | flops 13107200 | bytes 39331840 | tf_op jit(solution)/shard_map/convert.1
  132.7 4.1 copy.26
  136.7 5.2 %reshape.454 = bf16[1280,8,48,2]{0,3,2,1:T(2,128)(2,1)} reshape(bf16[8,160,768]{1,0,2:T(8,128)(2,1)S(1)} %copy.26) | data formatting | bytes 3932160 | tf_op jit(solution)/shard_map/reshape | solution.py:80
  142.0 8.9 %fusion.12 = bf16[8,48,2560]{2,1,0:T(8,128)(2,1)S(1)} fusion(bf16[1280,1,2560]{2,0,1:T(8,128)(2,1)} %get-tuple-element.28, bf16[1280,1,2560]{2,0,1:T(8,128)(2,1)} %get-tuple-element.29, bf16[1280,8,48,2]{0,3,2,1:T(2,128)(2,1)} %reshape.454), kind=kOutput, calls=%fused_computation.27 | convolution fusion | flops 5040701440 | bytes 17039360 | tf_op jit(solution)/shard_map/glkc,gcn->lkn/dot_general | solution.py:83
  150.9 5.4 %copy.31 = bf16[8,48,2560]{1,0,2:T(8,128)(2,1)} copy(bf16[8,48,2560]{2,1,0:T(8,128)(2,1)S(1)} %fusion.12) | data formatting | bytes 3932160 | tf_op jit(solution)/shard_map/convert_element_type | solution.py:85
  156.3 9.6 %reshape.471 = bf16[4,2,122880]{2,1,0:T(2,128)(2,1)} reshape(bf16[2560,8,48]{2,1,0:T(8,128)(2,1)} %bitcast.100) | data formatting | bytes 3932160
  165.9 4.5 %all-to-all-start.1 = ((bf16[4,2,122880]{2,1,0:T(2,128)(2,1)}), bf16[4,2,122880]{2,1,0:T(2,128)(2,1)S(1)}, u32[]{:S(2)}, u32[]{:S(2)}) async-start(bf16[4,2,122880]{2,1,0:T(2,128)(2,1)} %reshape.471), calls=%async_computation.1 | async-start | bytes 3932160 | tf_op jit(solution)/shard_map/all_to_all | solution.py:86
  172.3 21.5 %all-to-all-done.1 = bf16[4,2,122880]{2,1,0:T(2,128)(2,1)S(1)} async-done(((bf16[4,2,122880]{2,1,0:T(2,128)(2,1)}), bf16[4,2,122880]{2,1,0:T(2,128)(2,1)S(1)}, u32[]{:S(2)}, u32[]{:S(2)}) %all-to-all-start.1) | async-done | bytes 1966112 | tf_op jit(solution)/shard_map/all_to_all | solution.py:86
  193.9 6.3 %reshape.472 = bf16[2560,8,48]{2,1,0:T(8,128)(2,1)} reshape(bf16[4,2,122880]{2,1,0:T(2,128)(2,1)S(1)} %all-to-all-done.1) | data formatting | bytes 3932160
  200.1 5.7 %copy.32 = bf16[8,48,4,640]{3,1,2,0:T(8,128)(2,1)S(1)} copy(bf16[8,48,4,640]{1,0,3,2:T(8,128)(2,1)} %bitcast.101) | data formatting | bytes 3932160 | tf_op jit(solution)/shard_map/all_to_all | solution.py:86
  205.9 3.8 multiply_convert_fusion.2
  212.0 8.7 %convert_reduce_fusion = (f32[512]{0:T(512)S(1)}, bf16[8,640,512]{2,1,0:T(8,128)(2,1)S(1)}) fusion(f32[8,640,512]{2,1,0:T(8,128)S(1)} %get-tuple-element.25, f32[512]{0:T(512)S(1)} %copy-done.6, bf16[8,192,640]{2,1,0:T(8,128)(2,1)S(1)} %copy-done.3, bf16[512,192]{0,1:T(8,128)(2,1)S(1)} %copy-done.5), kind=kOutput, calls=%fused_computation.21 | convolution fusion | flops 1066925568 | bytes 17895424 | tf_op jit(solution)/shard_map/lkc,hk->lch/dot_general | solution.py:100
  225.2 4.3 convert_bitcast_fusion
  230.7 32.5 %all_to_all.68 = bf16[8,192,640]{2,0,1:T(8,128)(2,1)S(1)} all-to-all(bf16[8,192,640]{2,0,1:T(8,128)(2,1)S(1)} %copy.33), channel_id=1, replica_groups=mesh['lat'=8,'lon'=4] {'lon'}, dimensions={1} | all-to-all | bytes 3932160 | tf_op jit(solution)/shard_map/all_to_all | solution.py:129
  266.9 9.0 %fusion.14 = bf16[1280,8,48,2]{0,2,3,1:T(8,128)(2,1)S(1)} fusion(bf16[1280,1,2560]{2,0,1:T(8,128)(2,1)} %get-tuple-element.28, bf16[1280,1,2560]{2,0,1:T(8,128)(2,1)} %get-tuple-element.29, bf16[8,48,2560,1]{2,1,0,3:T(8,128)(2,1)} %reshape.466), kind=kOutput, calls=%fused_computation.31 | convolution fusion | flops 5060362240 | bytes 17039360 | tf_op jit(solution)/shard_map/gcn,lkn->glkc/dot_general | solution.py:130
  278.7 6.4 %all_to_all.61 = bf16[8,160,768]{1,0,2:T(8,128)(2,1)S(1)} reshape(bf16[1280,8,48,2]{0,3,2,1:T(2,128)(2,1)} %copy.35) | data formatting | bytes 3932160 | tf_op jit(solution)/shard_map/all_to_all | solution.py:134
  288.4 6.5 %all-to-all-start.3 = ((bf16[8,160,768]{2,1,0:T(8,128)(2,1)}), bf16[8,160,768]{2,1,0:T(8,128)(2,1)S(1)}, u32[]{:S(2)}, u32[]{:S(2)}) async-start(bf16[8,160,768]{2,1,0:T(8,128)(2,1)} %copy.36), calls=%async_computation.3 | async-start | bytes 3932160 | tf_op jit(solution)/shard_map/all_to_all | solution.py:134
  294.9 5.6 %fusion.23 = bf16[8,192,640]{2,1,0:T(8,128)(2,1)} fusion(f32[192]{0:T(256)S(1)} %copy-done.7, bf16[8,640,512]{2,1,0:T(8,128)(2,1)} %copy-done.8, bf16[512,192]{0,1:T(8,128)(2,1)S(1)} %copy-done.5), kind=kOutput, calls=%fused_computation.41 | convolution fusion | flops 1008599040 | bytes 7406336 | tf_op jit(solution)/shard_map/lch,hk->lkc/dot_general | solution.py:93
  300.5 75.0 %all-to-all-done.3 = bf16[8,160,768]{2,1,0:T(8,128)(2,1)S(1)} async-done(((bf16[8,160,768]{2,1,0:T(8,128)(2,1)}), bf16[8,160,768]{2,1,0:T(8,128)(2,1)S(1)}, u32[]{:S(2)}, u32[]{:S(2)}) %all-to-all-start.3) | async-done | bytes 1966112 | tf_op jit(solution)/shard_map/all_to_all | solution.py:134
  377.9 4.6 %reshape.456 = bf16[80,2,64,96]{3,2,1,0:T(8,128)(2,1)S(1)} reshape(bf16[160,8,768]{2,1,0:T(8,128)(2,1)} %copy.37) | data formatting | bytes 3932160 | tf_op jit(solution)/shard_map/reshape | solution.py:135
  384.8 3.5 rev.8
  388.3 20.7 %bitcast_convert_fusion = bf16[80,96,1408]{2,1,0:T(8,128)(2,1)} fusion(bf16[80,1,64,1408]{3,2,1,0:T(8,128)(2,1)} %get-tuple-element.7, bf16[80,1,64,1408]{3,2,1,0:T(8,128)(2,1)} %get-tuple-element.6, bf16[80,2,32,96]{3,2,1,0:T(8,128)(2,1)S(1)} %rev.8, bf16[80,2,32,96]{3,2,1,0:T(8,128)(2,1)} %get-tuple-element.8), kind=kOutput, calls=%fused_computation | convolution fusion | flops 2797404160 | bytes 52428800 | tf_op jit(solution)/shard_map/pqlk,pqlj->pkj/dot_general | solution.py:139
  409.0 9.9 %all-gather.4.cloned.1.call-done = f32[32,386,512]{2,1,0:T(8,128)} async-done(((f32[1,386,512]{2,1,0:T(8,128)}), f32[32,386,512]{2,1,0:T(8,128)}) %all-gather.4.cloned.1.call-update) | async-done | bytes 25296912 | tf_op jit(solution)/shard_map/all_gather | solution.py:8
  418.9 10.1 %reduce_sum.29 = f32[386,512]{1,0:T(8,128)S(1)} reduce(f32[32,386,512]{2,1,0:T(8,128)} %all-gather.4.cloned.1.call-done, f32[]{:T(128)} %constant.77.clone.1), dimensions={0}, to_apply=%region_2.3 | reduce | flops 6126592 | bytes 26087428 | tf_op jit(solution)/shard_map/reduce_sum | solution.py:8
  (58 shorter events, 44.7 us)
Async XLA Ops:
  7.2 198.7 %copy-start = (bf16[192,512]{1,0:T(8,128)(2,1)S(1)}, bf16[192,512]{1,0:T(8,128)(2,1)}, u32[]{:S(2)}) copy-start(bf16[192,512]{1,0:T(8,128)(2,1)} %param.11) | copy-start | bytes 589828
  8.3 7.3 %slice-start = ((s8[7208960]{0:T(1024)(128)(4,1)}), s8[4194304]{0:T(1024)(128)(4,1)S(1)}, s32[]{:S(2)}) async-start(s8[7208960]{0:T(1024)(128)(4,1)} %bitcast.97), calls=%async_computation.5 | async-start | bytes 8388608
  8.6 7.1 %slice-start.1 = ((s8[7208960]{0:T(1024)(128)(4,1)}), s8[3014656]{0:T(1024)(128)(4,1)S(1)}, s32[]{:S(2)}) async-start(s8[7208960]{0:T(1024)(128)(4,1)} %bitcast.97), calls=%async_computation.6 | async-start | bytes 6029312
  58.2 13.3 %copy-start.4 = (s32[640]{0:T(1024)S(1)}, s32[640]{0:T(1024)}, u32[]{:S(2)}) copy-start(s32[640]{0:T(1024)} %param.8) | copy-start | bytes 7684
  64.6 66.8 %all-to-all-start = ((bf16[160,8,768]{2,0,1:T(8,128)(2,1)}), bf16[160,8,768]{2,0,1:T(8,128)(2,1)S(1)}, u32[]{:S(2)}, u32[]{:S(2)}) async-start(bf16[160,8,768]{2,0,1:T(8,128)(2,1)} %copy.25), calls=%async_computation | async-start | bytes 3932160 | tf_op jit(solution)/shard_map/all_to_all | solution.py:78
  131.4 1.3 copy-start.1
  165.9 28.0 %all-to-all-start.1 = ((bf16[4,2,122880]{2,1,0:T(2,128)(2,1)}), bf16[4,2,122880]{2,1,0:T(2,128)(2,1)S(1)}, u32[]{:S(2)}, u32[]{:S(2)}) async-start(bf16[4,2,122880]{2,1,0:T(2,128)(2,1)} %reshape.471), calls=%async_computation.1 | async-start | bytes 3932160 | tf_op jit(solution)/shard_map/all_to_all | solution.py:86
  170.4 248.5 %all-gather.4.cloned.1.call-start = ((), (), s32[]{:S(2)}) async-start(), calls=%async_computation.4 | async-start | bytes 26492928 | tf_op jit(solution)/shard_map/all_gather | solution.py:8
  172.3 33.5 %copy-start.6 = (f32[512]{0:T(512)S(1)}, f32[512]{0:T(512)}, u32[]{:S(2)}) copy-start(f32[512]{0:T(512)} %param.12) | copy-start | bytes 6148
  205.9 3.9 copy-start.3
  209.7 2.3 copy-start.8
  209.7 2.3 copy-start.5
  220.7 2.4 copy-start.2
  278.7 16.2 %copy-start.7 = (f32[192]{0:T(256)S(1)}, f32[192]{0:T(256)}, u32[]{:S(2)}) copy-start(f32[192]{0:T(256)} %param.14) | copy-start | bytes 2308
  288.4 87.2 %all-to-all-start.3 = ((bf16[8,160,768]{2,1,0:T(8,128)(2,1)}), bf16[8,160,768]{2,1,0:T(8,128)(2,1)S(1)}, u32[]{:S(2)}, u32[]{:S(2)}) async-start(bf16[8,160,768]{2,1,0:T(8,128)(2,1)} %copy.36), calls=%async_computation.3 | async-start | bytes 3932160 | tf_op jit(solution)/shard_map/all_to_all | solution.py:134
Sparse Core Ops, SparseCore 0:
  225.3 193.5 all-gather.3
